TPU v7x, 32 devices: a whole 2x2x4 slice. The times are simulated.
32 devices in a mesh: dp: 4 (over y, x), feat: 8 (over z, core).
Axes of the slice: x: 2, y: 2, z: 4, core: 2. Of those that a mesh axis runs over, the one named last changes fastest.
Arguments:
- features: bfloat16 [8192, 1024], P('dp', 'feat'), may hold values from -6 to 6
- owners: int32 [8, 64, 1], P('feat', 'dp'), may hold values from 0 to 3; in each aligned block of 16 rows (0 to 15, 16 to 31, ..., all dimensions but the last counted through in order) at most 8 rows name the same one
- weights: bfloat16 [8, 4096], P(None, ('dp', 'feat')), may hold values from -0.1875 to 0.1875
- labels: int32 [8192], P('dp'), may hold values from 0 to 7
Outputs:
- hessian: float32 [32, 1024, 1024], P(('dp', 'feat'))
- gradient: float32 [8, 4096], P(None, ('dp', 'feat'))
Inputs may be any that keep to these rules, and one draw needn't show every extreme that they name: `owners`: among the 16 row blocks of one index of dp, in one tile column, at most 8 name the same owner, a bound that some block reaches.
All inputs are finite; a program needn't handle non-finite values.
Results may differ from a plain program's by a relative error of at most 0.0023.
Values may be sent and summed in bfloat16 or wider, within the bound.
A program may use at most 64 MiB of HBM per device.

v0:
```python
import math
import jax
import jax.numpy as jnp
from jax import lax
from jax.sharding import PartitionSpec as P


def normalize(logits):
    expo = jnp.exp(logits)
    return expo / jnp.sum(expo, axis=-1, keepdims=True)


def spread_diagonal(diag_part, classes, width):
    blocks = diag_part.reshape(classes, width, width)
    unit = jnp.eye(classes, dtype=jnp.float32)
    return (unit[:, None, :, None] * blocks[:, :, None, :]).reshape(
        classes * width, classes * width
    )


def arrange(target, groups, capacity):
    count = target.shape[0]
    order = jnp.arange(count, dtype=jnp.int32)
    earlier = (order[None, :] < order[:, None]) & (target[None, :] == target[:, None])
    ranking = jnp.sum(earlier.astype(jnp.int32), axis=1)
    slot_index = jnp.arange(groups * capacity, dtype=jnp.int32)
    slot_group = slot_index // capacity
    slot_rank = slot_index % capacity
    hits = (target[None, :] == slot_group[:, None]) & (ranking[None, :] == slot_rank[:, None])
    source = jnp.sum(jnp.where(hits, order[None, :], 0), axis=1)
    filled = jnp.any(hits, axis=1)
    return (source, filled)


def select_blocks(block_data, source, filled):
    picked = jnp.take(block_data, source, axis=0)
    return jnp.where(filled[:, None, None], picked, jnp.zeros_like(picked))


def accumulate(totals, feature_rows, prob_rows, classes):
    count, width = feature_rows.shape
    group = math.gcd(count, 512)

    def turn(step, state):
        hess_acc, grad_acc = state
        begin = step * group
        x_part = lax.dynamic_slice_in_dim(feature_rows, begin, group, 0)
        p_part = lax.dynamic_slice_in_dim(prob_rows, begin, group, 0)
        probs = p_part[:, :classes].astype(jnp.float32)
        resid = p_part[:, classes:]
        kron_rows = (
            (probs[:, :, None] * x_part.astype(jnp.float32)[:, None, :])
            .reshape(group, classes * width)
            .astype(jnp.bfloat16)
        )
        joint = jnp.concatenate([kron_rows, x_part], axis=1)
        product = lax.dot_general(
            kron_rows, joint, (((0,), (0,)), ((), ())), preferred_element_type=jnp.float32
        )
        square = product[:, : classes * width]
        diag_part = product[:, classes * width :]
        grad_term = lax.dot_general(
            resid, x_part, (((0,), (0,)), ((), ())), preferred_element_type=jnp.float32
        )
        return (
            hess_acc + spread_diagonal(diag_part, classes, width) - square,
            grad_acc + grad_term,
        )

    return lax.fori_loop(0, count // group, turn, totals)


def per_device(features, owners, weights, labels):
    rows, width = features.shape
    classes = weights.shape[0]
    blocks = owners.shape[1]
    block_rows = rows // blocks
    dp_count = lax.axis_size("dp")
    capacity = max(2, 2 * ((blocks + dp_count - 1) // dp_count))
    target = owners.reshape(blocks)
    gathered = lax.all_gather(weights, "dp", axis=1, tiled=True)
    table = gathered.reshape(classes, dp_count, width)
    every_owner = jnp.einsum("rt,cut->ruc", features, table, preferred_element_type=jnp.float32)
    row_owner = jnp.repeat(target, block_rows)
    owner_mask = (row_owner[:, None] == jnp.arange(dp_count, dtype=jnp.int32)[None, :]).astype(
        jnp.float32
    )
    partial_logits = jnp.sum(every_owner * owner_mask[:, :, None], axis=1)
    logits = lax.psum(partial_logits, "feat")
    probs = normalize(logits)
    onehot = (labels[:, None] == jnp.arange(classes, dtype=jnp.int32)[None, :]).astype(jnp.float32)
    probs_half = probs.astype(jnp.bfloat16)
    resid = (probs - onehot).astype(jnp.bfloat16)
    paired = jnp.concatenate([probs_half, resid], axis=1)
    feature_blocks = features.reshape(blocks, block_rows, width)
    paired_blocks = paired.reshape(blocks, block_rows, 2 * classes)
    start = (
        jnp.zeros((classes * width, classes * width), jnp.float32),
        jnp.zeros((classes, width), jnp.float32),
    )
    source, filled = arrange(target, dp_count, capacity)
    sent_features = select_blocks(feature_blocks, source, filled)
    sent_paired = select_blocks(paired_blocks, source, filled)
    got_features, got_paired = (
        lax.all_to_all(sent_features, "dp", split_axis=0, concat_axis=0, tiled=True),
        lax.all_to_all(sent_paired, "dp", split_axis=0, concat_axis=0, tiled=True),
    )
    hess_acc, grad_acc = accumulate(
        start, got_features.reshape(-1, width), got_paired.reshape(-1, 2 * classes), classes
    )
    hessian = (hess_acc / block_rows)[None]
    gradient = grad_acc / block_rows
    return (hessian, gradient)


def solution(mesh):
    in_specs = (P("dp", "feat"), P("feat", "dp", None), P(None, ("dp", "feat")), P("dp"))
    out_specs = (P(("dp", "feat"), None, None), P(None, ("dp", "feat")))
    return jax.shard_map(
        per_device, mesh=mesh, in_specs=in_specs, out_specs=out_specs, check_vma=False
    )
```

profile of v0, /device:TPU:0, one launch (start us, length us, event | category | flops | bytes accessed | tf_op | source)
XLA Modules:
  0.0 189.6 jit_solution(15932147110795025760)
XLA Ops:
  7.2 0.8 broadcast_bitcast_fusion
  8.0 9.6 %all_gather.3 = bf16[8,512]{1,0:T(8,128)(2,1)S(1)} all-gather(bf16[8,128]{1,0:T(8,128)(2,1)} %param.8), channel_id=1, replica_groups=mesh['dp'=4,'feat'=8] {'dp'}, dimensions={1}, use_global_device_ids=true | all-gather | bytes 10240 | tf_op jit(solution)/shard_map/all_gather | solution.py:81
  17.7 0.9 fusion.9
  18.6 0.9 convert_reduce_fusion
  19.5 0.7 select_reduce_fusion
  20.2 0.7 fusion.15
  21.0 0.7 gather_fusion.1
  21.8 50.8 %all-reduce.2.cloned.1.call-done = f32[2048,8]{0,1:T(8,128)} async-done(((f32[2048,8]{0,1:T(8,128)}), f32[2048,8]{0,1:T(8,128)}) %all-reduce.2.cloned.1.call-update) | async-done | bytes 65552 | tf_op jit(solution)/shard_map/psum | solution.py:89
  72.6 0.9 exponential_reduce_fusion
  73.5 0.9 fusion.12
  74.4 0.6 gather_fusion
  75.0 0.8 select_select_fusion.1
  75.8 3.6 %all-to-all-start = ((bf16[32,128,16]{1,2,0:T(8,128)(2,1)}), bf16[32,128,16]{1,2,0:T(8,128)(2,1)S(1)}, u32[]{:S(2)}, u32[]{:S(2)}) async-start(bf16[32,128,16]{1,2,0:T(8,128)(2,1)} %select_select_fusion.1), calls=%async_computation | async-start | bytes 262144 | tf_op jit(solution)/shard_map/all_to_all | solution.py:106
  79.4 1.2 select_select_fusion
  80.6 3.8 %all-to-all-done = bf16[32,128,16]{1,2,0:T(8,128)(2,1)S(1)} async-done(((bf16[32,128,16]{1,2,0:T(8,128)(2,1)}), bf16[32,128,16]{1,2,0:T(8,128)(2,1)S(1)}, u32[]{:S(2)}, u32[]{:S(2)}) %all-to-all-start) | async-done | bytes 131104 | tf_op jit(solution)/shard_map/all_to_all | solution.py:106
  84.4 3.5 %all-to-all-start.1 = ((bf16[32,128,128]{2,1,0:T(8,128)(2,1)}), bf16[32,128,128]{2,1,0:T(8,128)(2,1)S(1)}, u32[]{:S(2)}, u32[]{:S(2)}) async-start(bf16[32,128,128]{2,1,0:T(8,128)(2,1)} %select_select_fusion), calls=%async_computation.1 | async-start | bytes 2097152 | tf_op jit(solution)/shard_map/all_to_all | solution.py:105
  88.0 10.9 %all-to-all-done.1 = bf16[32,128,128]{2,1,0:T(8,128)(2,1)S(1)} async-done(((bf16[32,128,128]{2,1,0:T(8,128)(2,1)}), bf16[32,128,128]{2,1,0:T(8,128)(2,1)S(1)}, u32[]{:S(2)}, u32[]{:S(2)}) %all-to-all-start.1) | async-done | bytes 1048608 | tf_op jit(solution)/shard_map/all_to_all | solution.py:105
  98.9 78.2 %while.16 = (s32[]{:T(128)}, f32[1024,1024]{1,0:T(8,128)}, f32[8,128]{1,0:T(8,128)S(1)}, bf16[4096,16]{0,1:T(8,128)(2,1)S(1)}, bf16[4096,128]{1,0:T(8,128)(2,1)S...) while((s32[]{:T(128)}, f32[1024,1024]{1,0:T(8,128)}, f32[8,128]{1,0:T(8,128)S(1)}, ...), condition=%wide.region_7.8_spmd.clone, body=%wide.region_6.7_spmd.clone.sunk | while | flops 1216682112 | bytes 66151160 | solution.py:70
  99.2 0.7 multiply_convert_fusion.2
  100.2 1.6 fusion.34
  101.8 0.4 broadcast_multiply_fusion.3
  102.2 1.8 copy-done.1
  103.9 2.7 %fusion.36 = f32[1024,1024]{1,0:T(8,128)S(1)} fusion(f32[128,8,8,128]{3,2,1,0:T(8,128)S(1)} %bitcast.61, f32[1024,1152]{1,0:T(8,128)S(1)} %fusion.34, f32[1024,1024]{1,0:T(8,128)S(1)} %copy-done.1, pred[]{:T(512)S(6)} %compare.8), kind=kLoop, calls=%fused_computation.3.clone.1 | loop fusion | flops 3145728 | bytes 16777216 | tf_op jit(solution)/shard_map/while/body/eval_jaxpr/sub | solution.py:66
  106.6 2.0 %copy-done.2 = f32[1024,1024]{1,0:T(8,128)} copy-done((f32[1024,1024]{1,0:T(8,128)}, f32[1024,1024]{1,0:T(8,128)S(1)}, u32[]{:S(2)}) %copy-start.2) | copy-done | bytes 4194328 | tf_op jit(solution)/shard_map/while
  109.0 0.7 multiply_convert_fusion.2
  109.9 1.6 fusion.34
  111.6 0.4 broadcast_multiply_fusion.3
  111.9 1.8 copy-done.1
  113.7 2.7 %fusion.36 = f32[1024,1024]{1,0:T(8,128)S(1)} fusion(f32[128,8,8,128]{3,2,1,0:T(8,128)S(1)} %bitcast.61, f32[1024,1152]{1,0:T(8,128)S(1)} %fusion.34, f32[1024,1024]{1,0:T(8,128)S(1)} %copy-done.1, pred[]{:T(512)S(6)} %compare.8), kind=kLoop, calls=%fused_computation.3.clone.1 | loop fusion | flops 3145728 | bytes 16777216 | tf_op jit(solution)/shard_map/while/body/eval_jaxpr/sub | solution.py:66
  116.4 2.0 %copy-done.2 = f32[1024,1024]{1,0:T(8,128)} copy-done((f32[1024,1024]{1,0:T(8,128)}, f32[1024,1024]{1,0:T(8,128)S(1)}, u32[]{:S(2)}) %copy-start.2) | copy-done | bytes 4194328 | tf_op jit(solution)/shard_map/while
  118.7 0.7 multiply_convert_fusion.2
  119.7 1.6 fusion.34
  121.4 0.4 broadcast_multiply_fusion.3
  121.7 1.8 copy-done.1
  123.5 2.7 %fusion.36 = f32[1024,1024]{1,0:T(8,128)S(1)} fusion(f32[128,8,8,128]{3,2,1,0:T(8,128)S(1)} %bitcast.61, f32[1024,1152]{1,0:T(8,128)S(1)} %fusion.34, f32[1024,1024]{1,0:T(8,128)S(1)} %copy-done.1, pred[]{:T(512)S(6)} %compare.8), kind=kLoop, calls=%fused_computation.3.clone.1 | loop fusion | flops 3145728 | bytes 16777216 | tf_op jit(solution)/shard_map/while/body/eval_jaxpr/sub | solution.py:66
  126.2 2.0 %copy-done.2 = f32[1024,1024]{1,0:T(8,128)} copy-done((f32[1024,1024]{1,0:T(8,128)}, f32[1024,1024]{1,0:T(8,128)S(1)}, u32[]{:S(2)}) %copy-start.2) | copy-done | bytes 4194328 | tf_op jit(solution)/shard_map/while
  128.5 0.7 multiply_convert_fusion.2
  129.5 1.6 fusion.34
  131.1 0.4 broadcast_multiply_fusion.3
  131.5 1.8 copy-done.1
  133.3 2.7 %fusion.36 = f32[1024,1024]{1,0:T(8,128)S(1)} fusion(f32[128,8,8,128]{3,2,1,0:T(8,128)S(1)} %bitcast.61, f32[1024,1152]{1,0:T(8,128)S(1)} %fusion.34, f32[1024,1024]{1,0:T(8,128)S(1)} %copy-done.1, pred[]{:T(512)S(6)} %compare.8), kind=kLoop, calls=%fused_computation.3.clone.1 | loop fusion | flops 3145728 | bytes 16777216 | tf_op jit(solution)/shard_map/while/body/eval_jaxpr/sub | solution.py:66
  136.0 2.0 %copy-done.2 = f32[1024,1024]{1,0:T(8,128)} copy-done((f32[1024,1024]{1,0:T(8,128)}, f32[1024,1024]{1,0:T(8,128)S(1)}, u32[]{:S(2)}) %copy-start.2) | copy-done | bytes 4194328 | tf_op jit(solution)/shard_map/while
  138.3 0.7 multiply_convert_fusion.2
  139.3 1.6 fusion.34
  141.3 1.8 copy-done.1
  143.1 2.7 %fusion.36 = f32[1024,1024]{1,0:T(8,128)S(1)} fusion(f32[128,8,8,128]{3,2,1,0:T(8,128)S(1)} %bitcast.61, f32[1024,1152]{1,0:T(8,128)S(1)} %fusion.34, f32[1024,1024]{1,0:T(8,128)S(1)} %copy-done.1, pred[]{:T(512)S(6)} %compare.8), kind=kLoop, calls=%fused_computation.3.clone.1 | loop fusion | flops 3145728 | bytes 16777216 | tf_op jit(solution)/shard_map/while/body/eval_jaxpr/sub | solution.py:66
  145.8 2.0 %copy-done.2 = f32[1024,1024]{1,0:T(8,128)} copy-done((f32[1024,1024]{1,0:T(8,128)}, f32[1024,1024]{1,0:T(8,128)S(1)}, u32[]{:S(2)}) %copy-start.2) | copy-done | bytes 4194328 | tf_op jit(solution)/shard_map/while
  148.1 0.7 multiply_convert_fusion.2
  149.1 1.6 fusion.34
  151.1 1.8 copy-done.1
  152.8 2.7 %fusion.36 = f32[1024,1024]{1,0:T(8,128)S(1)} fusion(f32[128,8,8,128]{3,2,1,0:T(8,128)S(1)} %bitcast.61, f32[1024,1152]{1,0:T(8,128)S(1)} %fusion.34, f32[1024,1024]{1,0:T(8,128)S(1)} %copy-done.1, pred[]{:T(512)S(6)} %compare.8), kind=kLoop, calls=%fused_computation.3.clone.1 | loop fusion | flops 3145728 | bytes 16777216 | tf_op jit(solution)/shard_map/while/body/eval_jaxpr/sub | solution.py:66
  155.5 2.0 %copy-done.2 = f32[1024,1024]{1,0:T(8,128)} copy-done((f32[1024,1024]{1,0:T(8,128)}, f32[1024,1024]{1,0:T(8,128)S(1)}, u32[]{:S(2)}) %copy-start.2) | copy-done | bytes 4194328 | tf_op jit(solution)/shard_map/while
  157.9 0.7 multiply_convert_fusion.2
  158.8 1.6 fusion.34
  160.9 1.8 copy-done.1
  162.6 2.7 %fusion.36 = f32[1024,1024]{1,0:T(8,128)S(1)} fusion(f32[128,8,8,128]{3,2,1,0:T(8,128)S(1)} %bitcast.61, f32[1024,1152]{1,0:T(8,128)S(1)} %fusion.34, f32[1024,1024]{1,0:T(8,128)S(1)} %copy-done.1, pred[]{:T(512)S(6)} %compare.8), kind=kLoop, calls=%fused_computation.3.clone.1 | loop fusion | flops 3145728 | bytes 16777216 | tf_op jit(solution)/shard_map/while/body/eval_jaxpr/sub | solution.py:66
  165.3 2.0 %copy-done.2 = f32[1024,1024]{1,0:T(8,128)} copy-done((f32[1024,1024]{1,0:T(8,128)}, f32[1024,1024]{1,0:T(8,128)S(1)}, u32[]{:S(2)}) %copy-start.2) | copy-done | bytes 4194328 | tf_op jit(solution)/shard_map/while
  167.7 0.7 multiply_convert_fusion.2
  168.6 1.6 fusion.34
  170.6 1.8 copy-done.1
  172.4 2.7 %fusion.36 = f32[1024,1024]{1,0:T(8,128)S(1)} fusion(f32[128,8,8,128]{3,2,1,0:T(8,128)S(1)} %bitcast.61, f32[1024,1152]{1,0:T(8,128)S(1)} %fusion.34, f32[1024,1024]{1,0:T(8,128)S(1)} %copy-done.1, pred[]{:T(512)S(6)} %compare.8), kind=kLoop, calls=%fused_computation.3.clone.1 | loop fusion | flops 3145728 | bytes 16777216 | tf_op jit(solution)/shard_map/while/body/eval_jaxpr/sub | solution.py:66
  175.1 2.0 %copy-done.2 = f32[1024,1024]{1,0:T(8,128)} copy-done((f32[1024,1024]{1,0:T(8,128)}, f32[1024,1024]{1,0:T(8,128)S(1)}, u32[]{:S(2)}) %copy-start.2) | copy-done | bytes 4194328 | tf_op jit(solution)/shard_map/while
  177.1 0.6 broadcast_multiply_fusion.1
  177.7 5.0 %multiply_bitcast_fusion = f32[1,1024,1024]{2,1,0:T(8,128)} fusion(f32[1024,1024]{1,0:T(8,128)} %get-tuple-element.97), kind=kLoop, calls=%fused_computation.18 | loop fusion | flops 1048576 | bytes 8388608 | tf_op jit(solution)/shard_map/broadcast_in_dim | solution.py:111
  (89 shorter events, 6.5 us)
Async XLA Ops:
  7.2 10.5 %copy-start = (bf16[2048,128]{1,0:T(8,128)(2,1)S(1)}, bf16[2048,128]{1,0:T(8,128)(2,1)}, u32[]{:S(2)}) copy-start(bf16[2048,128]{1,0:T(8,128)(2,1)} %param.6) | copy-start | bytes 1572868
  7.2 65.4 %all-reduce.2.cloned.1.call-start = ((), (), s32[]{:S(2)}) async-start(), calls=%async_computation.2 | async-start | bytes 131072 | tf_op jit(solution)/shard_map/psum | solution.py:89
  75.8 8.7 %all-to-all-start = ((bf16[32,128,16]{1,2,0:T(8,128)(2,1)}), bf16[32,128,16]{1,2,0:T(8,128)(2,1)S(1)}, u32[]{:S(2)}, u32[]{:S(2)}) async-start(bf16[32,128,16]{1,2,0:T(8,128)(2,1)} %select_select_fusion.1), calls=%async_computation | async-start | bytes 262144 | tf_op jit(solution)/shard_map/all_to_all | solution.py:106
  84.4 14.4 %all-to-all-start.1 = ((bf16[32,128,128]{2,1,0:T(8,128)(2,1)}), bf16[32,128,128]{2,1,0:T(8,128)(2,1)S(1)}, u32[]{:S(2)}, u32[]{:S(2)}) async-start(bf16[32,128,128]{2,1,0:T(8,128)(2,1)} %select_select_fusion), calls=%async_computation.1 | async-start | bytes 2097152 | tf_op jit(solution)/shard_map/all_to_all | solution.py:105
  101.7 2.2 %copy-start.1 = (f32[1024,1024]{1,0:T(8,128)S(1)}, f32[1024,1024]{1,0:T(8,128)}, u32[]{:S(2)}) copy-start(f32[1024,1024]{1,0:T(8,128)} %get-tuple-element.179) | copy-start | bytes 12582916 | tf_op jit(solution)/shard_map/while
  106.6 2.0 %copy-start.2 = (f32[1024,1024]{1,0:T(8,128)}, f32[1024,1024]{1,0:T(8,128)S(1)}, u32[]{:S(2)}) copy-start(f32[1024,1024]{1,0:T(8,128)S(1)} %fusion.36) | copy-start | bytes 12582916 | tf_op jit(solution)/shard_map/while
  111.5 2.2 %copy-start.1 = (f32[1024,1024]{1,0:T(8,128)S(1)}, f32[1024,1024]{1,0:T(8,128)}, u32[]{:S(2)}) copy-start(f32[1024,1024]{1,0:T(8,128)} %get-tuple-element.179) | copy-start | bytes 12582916 | tf_op jit(solution)/shard_map/while
  116.4 2.0 %copy-start.2 = (f32[1024,1024]{1,0:T(8,128)}, f32[1024,1024]{1,0:T(8,128)S(1)}, u32[]{:S(2)}) copy-start(f32[1024,1024]{1,0:T(8,128)S(1)} %fusion.36) | copy-start | bytes 12582916 | tf_op jit(solution)/shard_map/while
  121.3 2.2 %copy-start.1 = (f32[1024,1024]{1,0:T(8,128)S(1)}, f32[1024,1024]{1,0:T(8,128)}, u32[]{:S(2)}) copy-start(f32[1024,1024]{1,0:T(8,128)} %get-tuple-element.179) | copy-start | bytes 12582916 | tf_op jit(solution)/shard_map/while
  126.2 2.0 %copy-start.2 = (f32[1024,1024]{1,0:T(8,128)}, f32[1024,1024]{1,0:T(8,128)S(1)}, u32[]{:S(2)}) copy-start(f32[1024,1024]{1,0:T(8,128)S(1)} %fusion.36) | copy-start | bytes 12582916 | tf_op jit(solution)/shard_map/while
  131.1 2.2 %copy-start.1 = (f32[1024,1024]{1,0:T(8,128)S(1)}, f32[1024,1024]{1,0:T(8,128)}, u32[]{:S(2)}) copy-start(f32[1024,1024]{1,0:T(8,128)} %get-tuple-element.179) | copy-start | bytes 12582916 | tf_op jit(solution)/shard_map/while
  136.0 2.0 %copy-start.2 = (f32[1024,1024]{1,0:T(8,128)}, f32[1024,1024]{1,0:T(8,128)S(1)}, u32[]{:S(2)}) copy-start(f32[1024,1024]{1,0:T(8,128)S(1)} %fusion.36) | copy-start | bytes 12582916 | tf_op jit(solution)/shard_map/while
  140.9 2.2 %copy-start.1 = (f32[1024,1024]{1,0:T(8,128)S(1)}, f32[1024,1024]{1,0:T(8,128)}, u32[]{:S(2)}) copy-start(f32[1024,1024]{1,0:T(8,128)} %get-tuple-element.179) | copy-start | bytes 12582916 | tf_op jit(solution)/shard_map/while
  145.8 2.0 %copy-start.2 = (f32[1024,1024]{1,0:T(8,128)}, f32[1024,1024]{1,0:T(8,128)S(1)}, u32[]{:S(2)}) copy-start(f32[1024,1024]{1,0:T(8,128)S(1)} %fusion.36) | copy-start | bytes 12582916 | tf_op jit(solution)/shard_map/while
  150.6 2.2 %copy-start.1 = (f32[1024,1024]{1,0:T(8,128)S(1)}, f32[1024,1024]{1,0:T(8,128)}, u32[]{:S(2)}) copy-start(f32[1024,1024]{1,0:T(8,128)} %get-tuple-element.179) | copy-start | bytes 12582916 | tf_op jit(solution)/shard_map/while
  155.5 2.0 %copy-start.2 = (f32[1024,1024]{1,0:T(8,128)}, f32[1024,1024]{1,0:T(8,128)S(1)}, u32[]{:S(2)}) copy-start(f32[1024,1024]{1,0:T(8,128)S(1)} %fusion.36) | copy-start | bytes 12582916 | tf_op jit(solution)/shard_map/while
  160.4 2.2 %copy-start.1 = (f32[1024,1024]{1,0:T(8,128)S(1)}, f32[1024,1024]{1,0:T(8,128)}, u32[]{:S(2)}) copy-start(f32[1024,1024]{1,0:T(8,128)} %get-tuple-element.179) | copy-start | bytes 12582916 | tf_op jit(solution)/shard_map/while
  165.3 2.0 %copy-start.2 = (f32[1024,1024]{1,0:T(8,128)}, f32[1024,1024]{1,0:T(8,128)S(1)}, u32[]{:S(2)}) copy-start(f32[1024,1024]{1,0:T(8,128)S(1)} %fusion.36) | copy-start | bytes 12582916 | tf_op jit(solution)/shard_map/while
  170.2 2.2 %copy-start.1 = (f32[1024,1024]{1,0:T(8,128)S(1)}, f32[1024,1024]{1,0:T(8,128)}, u32[]{:S(2)}) copy-start(f32[1024,1024]{1,0:T(8,128)} %get-tuple-element.179) | copy-start | bytes 12582916 | tf_op jit(solution)/shard_map/while
  175.1 2.0 %copy-start.2 = (f32[1024,1024]{1,0:T(8,128)}, f32[1024,1024]{1,0:T(8,128)S(1)}, u32[]{:S(2)}) copy-start(f32[1024,1024]{1,0:T(8,128)S(1)} %fusion.36) | copy-start | bytes 12582916 | tf_op jit(solution)/shard_map/while
Sparse Core Ops, SparseCore 0:
  18.7 53.8 all-reduce.1
where the time goes:
time: 190 us
  waiting for transfers between devices  65.6 us (35%)
  other arithmetic  42.1 us (22%)
  local copies, waits for them, and re-layouts  35.8 us (19%)
  matrix products  14.6 us (8%)
  between operations  14.1 us (7%)
  blocking collectives  9.63 us (5%)
  starting transfers between devices  7.2 us (4%)
    psum x1, waiting for transfers between devices, per_device(): logits = lax.psum(partial_logits, 'feat')  50.8 us
    while x40, local copies, waits for them, and re-layouts  32.4 us
    sub x8, other arithmetic, turn(): hess_acc + spread_diagonal(diag_part, classes, width) - square  21.6 us
    dot_general x8, matrix products, turn(): lax.dot_general(kron_rows, joint, (((0,), (0,)), ((), ())), preferred_ele...  12.6 us
    all_to_all x1, waiting for transfers between devices, per_device(): lax.all_to_all(sent_features, 'dp', split_axis=0, concat_axis=0, tiled=True)  10.9 us
    all_gather x1, blocking collectives, per_device(): gathered = lax.all_gather(weights, 'dp', axis=1, tiled=True)  9.63 us
    convert_element_type x8, other arithmetic, turn(): kron_rows = (probs[:, :, None] * x_part.astype(jnp.float32)[:, None, :])....  5.53 us
    broadcast_in_dim x1, other arithmetic, per_device(): hessian = (hess_acc / block_rows)[None]  5.04 us
  transfers between devices with their start and end apart: 3, of which 3 were waited for; matrix products, arithmetic and copies ran while one was open for 2% of the time, Pallas kernels for 0%

commit v1 on v0

--- a/solution.py
+++ b/solution.py
@@ -3,6 +3,29 @@
 import jax.numpy as jnp
 from jax import lax
 from jax.sharding import PartitionSpec as P
+
+
+def in_blocks(shard, dim, count):
+    before, after = (shard.shape[:dim], shard.shape[dim + 1 :])
+    return jnp.moveaxis(shard.reshape(*before, count, -1, *after), dim, 0)
+
+
+def in_order(blocks, dim):
+    blocks = jnp.moveaxis(blocks, 0, dim)
+    shape = blocks.shape
+    return blocks.reshape(*shape[:dim], shape[dim] * shape[dim + 1], *shape[dim + 2 :])
+
+
+def rotated_exchange(array, axis, split_dim, concat_dim):
+    count, index = (lax.axis_size(axis), lax.axis_index(axis))
+    blocks = in_blocks(array, split_dim, count)
+    whole = blocks
+    for hop in range(1, count):
+        target, source = ((index + hop) % count, (index - hop) % count)
+        sent = lax.dynamic_index_in_dim(blocks, target, 0)
+        other = lax.ppermute(sent, axis, [(i, (i + hop) % count) for i in range(count)])
+        whole = lax.dynamic_update_slice_in_dim(whole, other, source, axis=0)
+    return in_order(whole, concat_dim)
 
 
 def normalize(logits):
@@ -102,7 +125,7 @@
     sent_features = select_blocks(feature_blocks, source, filled)
     sent_paired = select_blocks(paired_blocks, source, filled)
     got_features, got_paired = (
-        lax.all_to_all(sent_features, "dp", split_axis=0, concat_axis=0, tiled=True),
+        rotated_exchange(sent_features, "dp", 0, 0),
         lax.all_to_all(sent_paired, "dp", split_axis=0, concat_axis=0, tiled=True),
     )
     hess_acc, grad_acc = accumulate(

time: 190 us -> 183 us (0.963); the launches traced: 190 us -> 180 us
  waiting for transfers between devices: 65.6 us -> 54.8 us
    all_to_all x1 -> x0, waiting for transfers between devices: 10.9 us -> none  [per_device(): lax.all_to_all(sent_features, 'dp', split_axis=0, concat_axis=0, tiled=True)]
    ppermute x0 -> x3, starting transfers between devices: none -> 4.96 us  [rotated_exchange(): lax.ppermute(sent, axis, [(i, (i + hop) % count) for i in range(count)])]
    ppermute x0 -> x3, waiting for transfers between devices: none -> 4.05 us  [rotated_exchange(): lax.ppermute(sent, axis, [(i, (i + hop) % count) for i in range(count)])]
    all_to_all x1 -> x0, starting transfers between devices: 3.52 us -> none  [per_device(): lax.all_to_all(sent_features, 'dp', split_axis=0, concat_axis=0, tiled=True)]
    all_to_all x1, waiting for transfers between devices: 3.82 us -> 1.75 us  [per_device(): lax.all_to_all(sent_paired, 'dp', split_axis=0, concat_axis=0, tiled=True)]
  transfers between devices with their start and end apart: 3 -> 5, of which waited for: 3 -> 3; matrix products, arithmetic and copies ran while one was open for 2% -> 4% of each run, Pallas kernels for 0% -> 0%
where the time goes in v1:
time: 183 us; the launch traced here: 180 us
  waiting for transfers between devices  54.8 us (30%)
  other arithmetic  41.1 us (22%)
  local copies, waits for them, and re-layouts  36.2 us (20%)
  matrix products  14.6 us (8%)
  between operations  14.2 us (8%)
  blocking collectives  9.63 us (5%)
  starting transfers between devices  8.65 us (5%)
    psum x1, waiting for transfers between devices, per_device(): logits = lax.psum(partial_logits, 'feat')  49 us
    while x40, local copies, waits for them, and re-layouts  32.4 us
    sub x8, other arithmetic, turn(): hess_acc + spread_diagonal(diag_part, classes, width) - square  21.6 us
    dot_general x8, matrix products, turn(): lax.dot_general(kron_rows, joint, (((0,), (0,)), ((), ())), preferred_ele...  12.6 us
    all_gather x1, blocking collectives, per_device(): gathered = lax.all_gather(weights, 'dp', axis=1, tiled=True)  9.63 us
    convert_element_type x8, other arithmetic, turn(): kron_rows = (probs[:, :, None] * x_part.astype(jnp.float32)[:, None, :])....  5.53 us
    broadcast_in_dim x1, other arithmetic, per_device(): hessian = (hess_acc / block_rows)[None]  5.04 us
    ppermute x3, starting transfers between devices, rotated_exchange(): lax.ppermute(sent, axis, [(i, (i + hop) % count) for i in range(count)])  4.96 us
  transfers between devices with their start and end apart: 5, of which 3 were waited for; matrix products, arithmetic and copies ran while one was open for 4% of the time, Pallas kernels for 0%

profile of v1, /device:TPU:0, one launch (start us, length us, event | category | flops | bytes accessed | tf_op | source)
XLA Modules:
  0.0 179.8 jit_solution(5247616607592729983)
XLA Ops:
  7.2 0.8 broadcast_bitcast_fusion
  8.0 9.6 %all_gather.3 = bf16[8,512]{1,0:T(8,128)(2,1)S(1)} all-gather(bf16[8,128]{1,0:T(8,128)(2,1)} %param.8), channel_id=1, replica_groups=mesh['dp'=4,'feat'=8] {'dp'}, dimensions={1}, use_global_device_ids=true | all-gather | bytes 10240 | tf_op jit(solution)/shard_map/all_gather | solution.py:104
  17.7 0.9 fusion.9
  18.6 0.9 convert_reduce_fusion
  19.5 0.7 select_reduce_fusion
  20.3 0.7 fusion.15
  21.2 0.7 gather_fusion.1
  22.2 1.4 collective-permute-start
  23.7 49.0 %all-reduce.2.cloned.1.call-done = f32[2048,8]{0,1:T(8,128)} async-done(((f32[2048,8]{0,1:T(8,128)}), f32[2048,8]{0,1:T(8,128)}) %all-reduce.2.cloned.1.call-update) | async-done | bytes 65552 | tf_op jit(solution)/shard_map/psum | solution.py:112
  72.6 0.9 exponential_reduce_fusion
  73.5 0.9 fusion.12
  74.4 0.6 gather_fusion
  75.0 0.8 select_select_fusion.1
  75.8 3.6 %all-to-all-start = ((bf16[32,128,16]{1,2,0:T(8,128)(2,1)}), bf16[32,128,16]{1,2,0:T(8,128)(2,1)S(1)}, u32[]{:S(2)}, u32[]{:S(2)}) async-start(bf16[32,128,16]{1,2,0:T(8,128)(2,1)} %select_select_fusion.1), calls=%async_computation | async-start | bytes 262144 | tf_op jit(solution)/shard_map/all_to_all | solution.py:129
  79.6 3.0 %collective-permute-start.2 = (bf16[1,8,128,128]{3,2,1,0:T(8,128)(2,1)S(1)}, bf16[1,8,128,128]{3,2,1,0:T(8,128)(2,1)S(1)}, u32[]{:S(2)}, u32[]{:S(2)}) collective-permute-start(bf16[1,8,128,128]{3,2,1,0:T(8,128)(2,1)S(1)} %get-tuple-element.129), channel_id=1, source_target_pairs={{0,24},{8,0},{16,8},{24,16},{1,25},{9,1},{17,9},{25,17},{2,26},{10... | collective-permute-start | bytes 786440 | tf_op jit(solution)/shard_map/ppermute | solution.py:26
  82.5 0.6 collective-permute-start.1
  83.1 1.7 all-to-all-done
  84.9 4.0 %collective-permute-done.1 = bf16[1,8,128,128]{3,2,1,0:T(8,128)(2,1)S(1)} collective-permute-done((bf16[1,8,128,128]{3,2,1,0:T(8,128)(2,1)S(1)}, bf16[1,8,128,128]{3,2,1,0:T(8,128)(2,1)S(1)}, u32[]{:S(2)}, u32[]{:S(2)}) %collective-permute-start.1) | collective-permute-done | bytes 262176 | tf_op jit(solution)/shard_map/ppermute | solution.py:26
  89.0 78.3 %while.16 = (s32[]{:T(128)}, f32[1024,1024]{1,0:T(8,128)}, f32[8,128]{1,0:T(8,128)S(1)}, bf16[4096,16]{0,1:T(8,128)(2,1)S(1)}, bf16[4096,128]{1,0:T(8,128)(2,1)S...) while((s32[]{:T(128)}, f32[1024,1024]{1,0:T(8,128)}, f32[8,128]{1,0:T(8,128)S(1)}, ...), condition=%wide.region_7.8_spmd.clone, body=%wide.region_6.7_spmd.clone.sunk | while | flops 1216682112 | bytes 66151160 | solution.py:93
  89.4 0.7 multiply_convert_fusion.2
  90.3 1.6 fusion.34
  92.0 0.4 broadcast_multiply_fusion.3
  92.3 1.8 copy-done.1
  94.1 2.7 %fusion.36 = f32[1024,1024]{1,0:T(8,128)S(1)} fusion(f32[128,8,8,128]{3,2,1,0:T(8,128)S(1)} %bitcast.62, f32[1024,1152]{1,0:T(8,128)S(1)} %fusion.34, f32[1024,1024]{1,0:T(8,128)S(1)} %copy-done.1, pred[]{:T(512)S(6)} %compare.14), kind=kLoop, calls=%fused_computation.3.clone.1 | loop fusion | flops 3145728 | bytes 16777216 | tf_op jit(solution)/shard_map/while/body/eval_jaxpr/sub | solution.py:89
  96.8 2.0 %copy-done.2 = f32[1024,1024]{1,0:T(8,128)} copy-done((f32[1024,1024]{1,0:T(8,128)}, f32[1024,1024]{1,0:T(8,128)S(1)}, u32[]{:S(2)}) %copy-start.2) | copy-done | bytes 4194328 | tf_op jit(solution)/shard_map/while
  99.1 0.7 multiply_convert_fusion.2
  100.1 1.6 fusion.34
  101.8 0.4 broadcast_multiply_fusion.3
  102.1 1.8 copy-done.1
  103.9 2.7 %fusion.36 = f32[1024,1024]{1,0:T(8,128)S(1)} fusion(f32[128,8,8,128]{3,2,1,0:T(8,128)S(1)} %bitcast.62, f32[1024,1152]{1,0:T(8,128)S(1)} %fusion.34, f32[1024,1024]{1,0:T(8,128)S(1)} %copy-done.1, pred[]{:T(512)S(6)} %compare.14), kind=kLoop, calls=%fused_computation.3.clone.1 | loop fusion | flops 3145728 | bytes 16777216 | tf_op jit(solution)/shard_map/while/body/eval_jaxpr/sub | solution.py:89
  106.6 2.0 %copy-done.2 = f32[1024,1024]{1,0:T(8,128)} copy-done((f32[1024,1024]{1,0:T(8,128)}, f32[1024,1024]{1,0:T(8,128)S(1)}, u32[]{:S(2)}) %copy-start.2) | copy-done | bytes 4194328 | tf_op jit(solution)/shard_map/while
  108.9 0.7 multiply_convert_fusion.2
  109.9 1.6 fusion.34
  111.5 0.4 broadcast_multiply_fusion.3
  111.9 1.8 copy-done.1
  113.7 2.7 %fusion.36 = f32[1024,1024]{1,0:T(8,128)S(1)} fusion(f32[128,8,8,128]{3,2,1,0:T(8,128)S(1)} %bitcast.62, f32[1024,1152]{1,0:T(8,128)S(1)} %fusion.34, f32[1024,1024]{1,0:T(8,128)S(1)} %copy-done.1, pred[]{:T(512)S(6)} %compare.14), kind=kLoop, calls=%fused_computation.3.clone.1 | loop fusion | flops 3145728 | bytes 16777216 | tf_op jit(solution)/shard_map/while/body/eval_jaxpr/sub | solution.py:89
  116.4 2.0 %copy-done.2 = f32[1024,1024]{1,0:T(8,128)} copy-done((f32[1024,1024]{1,0:T(8,128)}, f32[1024,1024]{1,0:T(8,128)S(1)}, u32[]{:S(2)}) %copy-start.2) | copy-done | bytes 4194328 | tf_op jit(solution)/shard_map/while
  118.7 0.7 multiply_convert_fusion.2
  119.7 1.6 fusion.34
  121.7 1.8 copy-done.1
  123.5 2.7 %fusion.36 = f32[1024,1024]{1,0:T(8,128)S(1)} fusion(f32[128,8,8,128]{3,2,1,0:T(8,128)S(1)} %bitcast.62, f32[1024,1152]{1,0:T(8,128)S(1)} %fusion.34, f32[1024,1024]{1,0:T(8,128)S(1)} %copy-done.1, pred[]{:T(512)S(6)} %compare.14), kind=kLoop, calls=%fused_computation.3.clone.1 | loop fusion | flops 3145728 | bytes 16777216 | tf_op jit(solution)/shard_map/while/body/eval_jaxpr/sub | solution.py:89
  126.2 2.0 %copy-done.2 = f32[1024,1024]{1,0:T(8,128)} copy-done((f32[1024,1024]{1,0:T(8,128)}, f32[1024,1024]{1,0:T(8,128)S(1)}, u32[]{:S(2)}) %copy-start.2) | copy-done | bytes 4194328 | tf_op jit(solution)/shard_map/while
  128.5 0.7 multiply_convert_fusion.2
  129.5 1.6 fusion.34
  131.5 1.8 copy-done.1
  133.2 2.7 %fusion.36 = f32[1024,1024]{1,0:T(8,128)S(1)} fusion(f32[128,8,8,128]{3,2,1,0:T(8,128)S(1)} %bitcast.62, f32[1024,1152]{1,0:T(8,128)S(1)} %fusion.34, f32[1024,1024]{1,0:T(8,128)S(1)} %copy-done.1, pred[]{:T(512)S(6)} %compare.14), kind=kLoop, calls=%fused_computation.3.clone.1 | loop fusion | flops 3145728 | bytes 16777216 | tf_op jit(solution)/shard_map/while/body/eval_jaxpr/sub | solution.py:89
  135.9 2.0 %copy-done.2 = f32[1024,1024]{1,0:T(8,128)} copy-done((f32[1024,1024]{1,0:T(8,128)}, f32[1024,1024]{1,0:T(8,128)S(1)}, u32[]{:S(2)}) %copy-start.2) | copy-done | bytes 4194328 | tf_op jit(solution)/shard_map/while
  138.3 0.7 multiply_convert_fusion.2
  139.2 1.6 fusion.34
  141.2 1.8 copy-done.1
  143.0 2.7 %fusion.36 = f32[1024,1024]{1,0:T(8,128)S(1)} fusion(f32[128,8,8,128]{3,2,1,0:T(8,128)S(1)} %bitcast.62, f32[1024,1152]{1,0:T(8,128)S(1)} %fusion.34, f32[1024,1024]{1,0:T(8,128)S(1)} %copy-done.1, pred[]{:T(512)S(6)} %compare.14), kind=kLoop, calls=%fused_computation.3.clone.1 | loop fusion | flops 3145728 | bytes 16777216 | tf_op jit(solution)/shard_map/while/body/eval_jaxpr/sub | solution.py:89
  145.7 2.0 %copy-done.2 = f32[1024,1024]{1,0:T(8,128)} copy-done((f32[1024,1024]{1,0:T(8,128)}, f32[1024,1024]{1,0:T(8,128)S(1)}, u32[]{:S(2)}) %copy-start.2) | copy-done | bytes 4194328 | tf_op jit(solution)/shard_map/while
  148.0 0.7 multiply_convert_fusion.2
  149.0 1.6 fusion.34
  151.0 1.8 copy-done.1
  152.8 2.7 %fusion.36 = f32[1024,1024]{1,0:T(8,128)S(1)} fusion(f32[128,8,8,128]{3,2,1,0:T(8,128)S(1)} %bitcast.62, f32[1024,1152]{1,0:T(8,128)S(1)} %fusion.34, f32[1024,1024]{1,0:T(8,128)S(1)} %copy-done.1, pred[]{:T(512)S(6)} %compare.14), kind=kLoop, calls=%fused_computation.3.clone.1 | loop fusion | flops 3145728 | bytes 16777216 | tf_op jit(solution)/shard_map/while/body/eval_jaxpr/sub | solution.py:89
  155.5 2.0 %copy-done.2 = f32[1024,1024]{1,0:T(8,128)} copy-done((f32[1024,1024]{1,0:T(8,128)}, f32[1024,1024]{1,0:T(8,128)S(1)}, u32[]{:S(2)}) %copy-start.2) | copy-done | bytes 4194328 | tf_op jit(solution)/shard_map/while
  157.8 0.7 multiply_convert_fusion.2
  158.8 1.6 fusion.34
  160.8 1.8 copy-done.1
  162.6 2.7 %fusion.36 = f32[1024,1024]{1,0:T(8,128)S(1)} fusion(f32[128,8,8,128]{3,2,1,0:T(8,128)S(1)} %bitcast.62, f32[1024,1152]{1,0:T(8,128)S(1)} %fusion.34, f32[1024,1024]{1,0:T(8,128)S(1)} %copy-done.1, pred[]{:T(512)S(6)} %compare.14), kind=kLoop, calls=%fused_computation.3.clone.1 | loop fusion | flops 3145728 | bytes 16777216 | tf_op jit(solution)/shard_map/while/body/eval_jaxpr/sub | solution.py:89
  165.3 2.0 %copy-done.2 = f32[1024,1024]{1,0:T(8,128)} copy-done((f32[1024,1024]{1,0:T(8,128)}, f32[1024,1024]{1,0:T(8,128)S(1)}, u32[]{:S(2)}) %copy-start.2) | copy-done | bytes 4194328 | tf_op jit(solution)/shard_map/while
  167.3 0.6 broadcast_multiply_fusion.1
  167.9 5.0 %multiply_bitcast_fusion = f32[1,1024,1024]{2,1,0:T(8,128)} fusion(f32[1024,1024]{1,0:T(8,128)} %get-tuple-element.97), kind=kLoop, calls=%fused_computation.18 | loop fusion | flops 1048576 | bytes 8388608 | tf_op jit(solution)/shard_map/broadcast_in_dim | solution.py:134
  (102 shorter events, 7.5 us)
Async XLA Ops:
  7.2 10.5 %copy-start = (bf16[2048,128]{1,0:T(8,128)(2,1)S(1)}, bf16[2048,128]{1,0:T(8,128)(2,1)}, u32[]{:S(2)}) copy-start(bf16[2048,128]{1,0:T(8,128)(2,1)} %param.6) | copy-start | bytes 1572868
  7.2 66.3 %copy-start.3 = (s32[2048]{0:T(1024)S(1)}, s32[2048]{0:T(1024)}, u32[]{:S(2)}) copy-start(s32[2048]{0:T(1024)} %param.9) | copy-start | bytes 24580
  7.2 65.4 %all-reduce.2.cloned.1.call-start = ((), (), s32[]{:S(2)}) async-start(), calls=%async_computation.1 | async-start | bytes 131072 | tf_op jit(solution)/shard_map/psum | solution.py:112
  22.2 57.2 %collective-permute-start = (bf16[1,8,128,128]{3,2,1,0:T(8,128)(2,1)S(1)}, bf16[1,8,128,128]{3,2,1,0:T(8,128)(2,1)S(1)}, u32[]{:S(2)}, u32[]{:S(2)}) collective-permute-start(bf16[1,8,128,128]{3,2,1,0:T(8,128)(2,1)S(1)} %constant_dynamic-slice_fusion.3), channel_id=1, source_target_pairs={{0,8},{8,16},{16,24},{24,0},{1,9},{9,17},{17,25},{25,1},{2,10},{10... | collective-permute-start | bytes 786440 | tf_op jit(solution)/shard_map/ppermute | solution.py:26
  75.8 9.1 %all-to-all-start = ((bf16[32,128,16]{1,2,0:T(8,128)(2,1)}), bf16[32,128,16]{1,2,0:T(8,128)(2,1)S(1)}, u32[]{:S(2)}, u32[]{:S(2)}) async-start(bf16[32,128,16]{1,2,0:T(8,128)(2,1)} %select_select_fusion.1), calls=%async_computation | async-start | bytes 262144 | tf_op jit(solution)/shard_map/all_to_all | solution.py:129
  79.6 9.4 %collective-permute-start.2 = (bf16[1,8,128,128]{3,2,1,0:T(8,128)(2,1)S(1)}, bf16[1,8,128,128]{3,2,1,0:T(8,128)(2,1)S(1)}, u32[]{:S(2)}, u32[]{:S(2)}) collective-permute-start(bf16[1,8,128,128]{3,2,1,0:T(8,128)(2,1)S(1)} %get-tuple-element.129), channel_id=1, source_target_pairs={{0,24},{8,0},{16,8},{24,16},{1,25},{9,1},{17,9},{25,17},{2,26},{10... | collective-permute-start | bytes 786440 | tf_op jit(solution)/shard_map/ppermute | solution.py:26
  82.5 6.4 %collective-permute-start.1 = (bf16[1,8,128,128]{3,2,1,0:T(8,128)(2,1)S(1)}, bf16[1,8,128,128]{3,2,1,0:T(8,128)(2,1)S(1)}, u32[]{:S(2)}, u32[]{:S(2)}) collective-permute-start(bf16[1,8,128,128]{3,2,1,0:T(8,128)(2,1)S(1)} %get-tuple-element.130), channel_id=1, source_target_pairs={{0,16},{8,24},{16,0},{24,8},{1,17},{9,25},{17,1},{25,9},{2,18},{10... | collective-permute-start | bytes 786440 | tf_op jit(solution)/shard_map/ppermute | solution.py:26
  91.9 2.2 %copy-start.1 = (f32[1024,1024]{1,0:T(8,128)S(1)}, f32[1024,1024]{1,0:T(8,128)}, u32[]{:S(2)}) copy-start(f32[1024,1024]{1,0:T(8,128)} %get-tuple-element.182) | copy-start | bytes 12582916 | tf_op jit(solution)/shard_map/while
  96.8 2.0 %copy-start.2 = (f32[1024,1024]{1,0:T(8,128)}, f32[1024,1024]{1,0:T(8,128)S(1)}, u32[]{:S(2)}) copy-start(f32[1024,1024]{1,0:T(8,128)S(1)} %fusion.36) | copy-start | bytes 12582916 | tf_op jit(solution)/shard_map/while
  101.7 2.2 %copy-start.1 = (f32[1024,1024]{1,0:T(8,128)S(1)}, f32[1024,1024]{1,0:T(8,128)}, u32[]{:S(2)}) copy-start(f32[1024,1024]{1,0:T(8,128)} %get-tuple-element.182) | copy-start | bytes 12582916 | tf_op jit(solution)/shard_map/while
  106.6 2.0 %copy-start.2 = (f32[1024,1024]{1,0:T(8,128)}, f32[1024,1024]{1,0:T(8,128)S(1)}, u32[]{:S(2)}) copy-start(f32[1024,1024]{1,0:T(8,128)S(1)} %fusion.36) | copy-start | bytes 12582916 | tf_op jit(solution)/shard_map/while
  111.5 2.2 %copy-start.1 = (f32[1024,1024]{1,0:T(8,128)S(1)}, f32[1024,1024]{1,0:T(8,128)}, u32[]{:S(2)}) copy-start(f32[1024,1024]{1,0:T(8,128)} %get-tuple-element.182) | copy-start | bytes 12582916 | tf_op jit(solution)/shard_map/while
  116.4 2.0 %copy-start.2 = (f32[1024,1024]{1,0:T(8,128)}, f32[1024,1024]{1,0:T(8,128)S(1)}, u32[]{:S(2)}) copy-start(f32[1024,1024]{1,0:T(8,128)S(1)} %fusion.36) | copy-start | bytes 12582916 | tf_op jit(solution)/shard_map/while
  121.3 2.2 %copy-start.1 = (f32[1024,1024]{1,0:T(8,128)S(1)}, f32[1024,1024]{1,0:T(8,128)}, u32[]{:S(2)}) copy-start(f32[1024,1024]{1,0:T(8,128)} %get-tuple-element.182) | copy-start | bytes 12582916 | tf_op jit(solution)/shard_map/while
  126.2 2.0 %copy-start.2 = (f32[1024,1024]{1,0:T(8,128)}, f32[1024,1024]{1,0:T(8,128)S(1)}, u32[]{:S(2)}) copy-start(f32[1024,1024]{1,0:T(8,128)S(1)} %fusion.36) | copy-start | bytes 12582916 | tf_op jit(solution)/shard_map/while
  131.0 2.2 %copy-start.1 = (f32[1024,1024]{1,0:T(8,128)S(1)}, f32[1024,1024]{1,0:T(8,128)}, u32[]{:S(2)}) copy-start(f32[1024,1024]{1,0:T(8,128)} %get-tuple-element.182) | copy-start | bytes 12582916 | tf_op jit(solution)/shard_map/while
  135.9 2.0 %copy-start.2 = (f32[1024,1024]{1,0:T(8,128)}, f32[1024,1024]{1,0:T(8,128)S(1)}, u32[]{:S(2)}) copy-start(f32[1024,1024]{1,0:T(8,128)S(1)} %fusion.36) | copy-start | bytes 12582916 | tf_op jit(solution)/shard_map/while
  140.8 2.2 %copy-start.1 = (f32[1024,1024]{1,0:T(8,128)S(1)}, f32[1024,1024]{1,0:T(8,128)}, u32[]{:S(2)}) copy-start(f32[1024,1024]{1,0:T(8,128)} %get-tuple-element.182) | copy-start | bytes 12582916 | tf_op jit(solution)/shard_map/while
  145.7 2.0 %copy-start.2 = (f32[1024,1024]{1,0:T(8,128)}, f32[1024,1024]{1,0:T(8,128)S(1)}, u32[]{:S(2)}) copy-start(f32[1024,1024]{1,0:T(8,128)S(1)} %fusion.36) | copy-start | bytes 12582916 | tf_op jit(solution)/shard_map/while
  150.6 2.2 %copy-start.1 = (f32[1024,1024]{1,0:T(8,128)S(1)}, f32[1024,1024]{1,0:T(8,128)}, u32[]{:S(2)}) copy-start(f32[1024,1024]{1,0:T(8,128)} %get-tuple-element.182) | copy-start | bytes 12582916 | tf_op jit(solution)/shard_map/while
  155.5 2.0 %copy-start.2 = (f32[1024,1024]{1,0:T(8,128)}, f32[1024,1024]{1,0:T(8,128)S(1)}, u32[]{:S(2)}) copy-start(f32[1024,1024]{1,0:T(8,128)S(1)} %fusion.36) | copy-start | bytes 12582916 | tf_op jit(solution)/shard_map/while
  160.4 2.2 %copy-start.1 = (f32[1024,1024]{1,0:T(8,128)S(1)}, f32[1024,1024]{1,0:T(8,128)}, u32[]{:S(2)}) copy-start(f32[1024,1024]{1,0:T(8,128)} %get-tuple-element.182) | copy-start | bytes 12582916 | tf_op jit(solution)/shard_map/while
  165.3 2.0 %copy-start.2 = (f32[1024,1024]{1,0:T(8,128)}, f32[1024,1024]{1,0:T(8,128)S(1)}, u32[]{:S(2)}) copy-start(f32[1024,1024]{1,0:T(8,128)S(1)} %fusion.36) | copy-start | bytes 12582916 | tf_op jit(solution)/shard_map/while
Sparse Core Ops, SparseCore 0:
  18.7 53.8 all-reduce.1
